TPU v7x, 128 devices: a whole 4x4x4 slice. The times are simulated.
128 devices in a mesh: row: 8 (over x, z_lo), col: 16 (over z_hi, y, core).
Axes of the slice: x: 4, y: 4, z: 4 (z_hi: 2, z_lo: 2; z = z_hi * 2 + z_lo), core: 2. Of those that a mesh axis runs over, the one named last changes fastest.
Arguments:
- pair: bfloat16 [512, 512, 128], P('row', 'col'), may hold values from -6 to 6
- cotangent: bfloat16 [512, 512, 128], P('row', 'col'), may hold values from -6 to 6
- res_mask: int32 [512], replicated, may hold values 0 or 1
- chain: int32 [512], replicated, may hold values from 0 to 3, never falling along the last dimension, each value on 1 to 256 neighbouring positions
- ln_in_gain: float32 [128], replicated, may hold values from 0.5 to 1.5
- ln_in_bias: float32 [128], replicated, may hold values from -3 to 3
- w_proj: bfloat16 [128, 512], replicated, may hold values from -0.5 to 0.5
- w_gate: bfloat16 [128, 128], replicated, may hold values from -0.5 to 0.5
- chain_bias: float32 [128], replicated, may hold values from -4 to 4
- ln_out_gain: float32 [128], replicated, may hold values from 0.5 to 1.5
- ln_out_bias: float32 [128], replicated, may hold values from -3 to 3
- w_out: bfloat16 [128, 128], replicated, may hold values from -0.5 to 0.5
Outputs:
- grad_pair: bfloat16 [512, 512, 128], P('row', 'col')
- grad_proj: float32 [128, 512], replicated
- grad_gate: float32 [128, 128], replicated
- grad_out: float32 [128, 128], replicated
Inputs may be any that keep to these rules, and one draw needn't show every extreme that they name: chain never decreases along the residues.
All inputs are finite; a program needn't handle non-finite values.
Results may differ from a plain program's by a relative error of at most 0.02.
Values may be sent and summed in bfloat16 or wider, within the bound.
No kernel may reach another device: no remote copies, remote signals or barrier semaphores. Data moves between devices by JAX's collectives and lax.ppermute only.
A program may use at most 128 MiB of HBM per device.

v0:
```python
import jax
import jax.numpy as jnp
from jax import lax
from jax.sharding import PartitionSpec as P

EPS = 1e-05


def layer_norm(values, gain, bias):
    mean = jnp.mean(values, axis=-1, keepdims=True)
    centred = values - mean
    inverse = lax.rsqrt(jnp.mean(centred * centred, axis=-1, keepdims=True) + EPS)
    normed = centred * inverse
    return (normed * gain + bias, normed, inverse)


def norm_back(grad_normed, normed, inverse):
    first = jnp.mean(grad_normed, axis=-1, keepdims=True)
    second = jnp.mean(grad_normed * normed, axis=-1, keepdims=True)
    return (grad_normed - first - normed * second) * inverse


def matmul_last(left, right):
    shape = left.shape
    flat = jnp.dot(left.reshape(-1, shape[-1]), right, preferred_element_type=jnp.float32)
    return flat.reshape(shape[:-1] + (right.shape[1],))


def contract_pairs(left, right):
    flat_left = left.reshape(-1, left.shape[-1])
    flat_right = right.reshape(-1, right.shape[-1])
    return lax.dot_general(
        flat_left, flat_right, (((0,), (0,)), ((), ())), preferred_element_type=jnp.float32
    )


def project(pair, ln_in_gain, ln_in_bias, w_proj):
    scaled, normed, inverse = layer_norm(pair.astype(jnp.float32), ln_in_gain, ln_in_bias)
    normed_b = scaled.astype(jnp.bfloat16)
    return (normed_b, normed, inverse, matmul_last(normed_b, w_proj))


def activations(proj, pair_mask):
    width = proj.shape[-1] // 4
    gate_a = jax.nn.sigmoid(proj[..., :width])
    gate_b = jax.nn.sigmoid(proj[..., 2 * width : 3 * width])
    act_a = (gate_a * proj[..., width : 2 * width] * pair_mask).astype(jnp.bfloat16)
    act_b = (gate_b * proj[..., 3 * width :] * pair_mask).astype(jnp.bfloat16)
    return (act_a, act_b)


def gated_output(
    mixed, cotangent, normed_b, same, chain_bias, w_gate, ln_out_gain, ln_out_bias, w_out
):
    scaled, normed, inverse = layer_norm(mixed, ln_out_gain, ln_out_bias)
    out_b = scaled.astype(jnp.bfloat16)
    update = matmul_last(out_b, w_out)
    gate = jax.nn.sigmoid(matmul_last(normed_b, w_gate) + same * chain_bias)
    cot = cotangent.astype(jnp.float32)
    grad_update = (cot * gate).astype(jnp.bfloat16)
    grad_logit = (cot * update * gate * (1.0 - gate)).astype(jnp.bfloat16)
    grad_scaled = matmul_last(grad_update, w_out.T)
    grad_mixed = norm_back(grad_scaled * ln_out_gain, normed, inverse).astype(jnp.bfloat16)
    return (
        grad_mixed,
        grad_logit,
        contract_pairs(out_b, grad_update),
        contract_pairs(normed_b, grad_logit),
    )


def input_back(
    normed_b,
    normed,
    inverse,
    proj,
    pair_mask,
    grad_a,
    grad_b,
    grad_logit,
    ln_in_gain,
    w_proj,
    w_gate,
):
    width = proj.shape[-1] // 4
    gate_a = jax.nn.sigmoid(proj[..., :width])
    gate_b = jax.nn.sigmoid(proj[..., 2 * width : 3 * width])
    masked_a = grad_a * pair_mask
    masked_b = grad_b * pair_mask
    grad_p = jnp.concatenate(
        [
            masked_a * proj[..., width : 2 * width] * gate_a * (1.0 - gate_a),
            masked_a * gate_a,
            masked_b * proj[..., 3 * width :] * gate_b * (1.0 - gate_b),
            masked_b * gate_b,
        ],
        axis=-1,
    ).astype(jnp.bfloat16)
    grad_zn = matmul_last(grad_p, w_proj.T) + matmul_last(grad_logit, w_gate.T)
    grad_pair = norm_back(grad_zn * ln_in_gain, normed, inverse).astype(jnp.bfloat16)
    return (grad_pair, contract_pairs(normed_b, grad_p))


def body(
    pair,
    cotangent,
    res_mask,
    chain,
    ln_in_gain,
    ln_in_bias,
    w_proj,
    w_gate,
    chain_bias,
    ln_out_gain,
    ln_out_bias,
    w_out,
):
    tile_rows = pair.shape[0]
    tile_cols = pair.shape[1]
    total = tile_rows * lax.axis_size("row")
    row_start = lax.axis_index("row") * tile_rows
    col_start = lax.axis_index("col") * tile_cols
    maskf = res_mask.astype(jnp.float32)
    mask_rows = lax.dynamic_slice_in_dim(maskf, row_start, tile_rows)
    mask_cols = lax.dynamic_slice_in_dim(maskf, col_start, tile_cols)
    pair_mask = mask_rows[:, None, None] * mask_cols[None, :, None]
    chain_rows = lax.dynamic_slice_in_dim(chain, row_start, tile_rows)
    chain_cols = lax.dynamic_slice_in_dim(chain, col_start, tile_cols)
    same = (chain_rows[:, None] == chain_cols[None, :]).astype(jnp.float32)[:, :, None]
    normed_b, normed, inverse, proj = project(pair, ln_in_gain, ln_in_bias, w_proj)
    act_a, act_b = activations(proj, pair_mask)
    b_cols = lax.all_gather(act_b, "row", axis=0, tiled=True)
    piece = b_cols
    mixed = jnp.transpose(
        lax.psum_scatter(
            jnp.einsum("ikh,jkh->jih", act_a, piece, preferred_element_type=jnp.float32).astype(
                jnp.bfloat16
            ),
            "col",
            scatter_dimension=0,
            tiled=True,
        ).astype(jnp.float32),
        (1, 0, 2),
    )
    grad_mixed, grad_logit, term_out, term_gate = gated_output(
        mixed, cotangent, normed_b, same, chain_bias, w_gate, ln_out_gain, ln_out_bias, w_out
    )
    dx_rows = lax.all_gather(grad_mixed, "col", axis=1, tiled=True)
    grad_a = jnp.einsum("ijh,jkh->ikh", dx_rows, b_cols, preferred_element_type=jnp.float32)
    piece = dx_rows
    grad_b = lax.psum_scatter(
        jnp.einsum("ijh,ikh->jkh", piece, act_a, preferred_element_type=jnp.float32).astype(
            jnp.bfloat16
        ),
        "row",
        scatter_dimension=0,
        tiled=True,
    ).astype(jnp.float32)
    grad_pair, term_proj = input_back(
        normed_b,
        normed,
        inverse,
        proj,
        pair_mask,
        grad_a,
        grad_b,
        grad_logit,
        ln_in_gain,
        w_proj,
        w_gate,
    )
    sums = lax.psum((term_proj, term_gate, term_out), ("row", "col"))
    scale = 1.0 / total
    return (grad_pair, sums[0] * scale, sums[1] * scale, sums[2] * scale)


def solution(mesh):
    return jax.shard_map(
        body,
        mesh=mesh,
        in_specs=(
            P("row", "col", None),
            P("row", "col", None),
            P(),
            P(),
            P(),
            P(),
            P(),
            P(),
            P(),
            P(),
            P(),
            P(),
        ),
        out_specs=(P("row", "col", None), P(), P(), P()),
        check_vma=False,
    )
```

profile of v0, /device:TPU:1, one launch (start us, length us, event | category | flops | bytes accessed | tf_op | source)
XLA Modules:
  0.0 634.5 jit_solution(537603368556544840)
XLA Ops:
  7.2 0.0 copy-start
  7.2 0.0 all-gather.3.cloned.1.call-start
  7.2 0.7 convert_element_type.61
  7.9 0.1 dynamic_slice.13
  8.0 0.1 dynamic_slice.12
  8.1 1.4 convert_reduce_fusion
  9.5 1.7 fusion.19
  11.2 0.1 broadcast_multiply_fusion.3
  11.2 2.0 fusion.42
  13.3 2.0 copy-done.2
  15.2 1.4 multiply_convert_fusion.4
  16.6 0.0 all-gather.3.cloned.1.call-update
  16.6 0.0 reduce-scatter.3.cloned.1.call-start
  16.7 1.7 copy.32
  18.4 91.4 %all-gather.3.cloned.1.call-done = bf16[512,32,128]{2,1,0:T(8,128)(2,1)} async-done(((bf16[64,32,128]{2,1,0:T(8,128)(2,1)}), bf16[512,32,128]{2,1,0:T(8,128)(2,1)}) %all-gather.3.cloned.1.call-update) | async-done | bytes 4194320 | tf_op jit(solution)/shard_map/all_gather | solution.py:132
  109.8 8.6 %copy.34 = bf16[512,32,128]{0,1,2:T(8,128)(2,1)} copy(bf16[512,32,128]{2,1,0:T(8,128)(2,1)} %all-gather.3.cloned.1.call-done) | data formatting | bytes 8388608 | tf_op jit(solution)/shard_map/all_gather | solution.py:132
  118.4 7.8 %fusion.59 = bf16[128,512,64]{1,2,0:T(8,128)(2,1)} fusion(bf16[512,32,128]{0,1,2:T(8,128)(2,1)} %copy.34, bf16[64,32,128]{0,1,2:T(8,128)(2,1)S(1)} %copy.32), kind=kOutput, calls=%fused_computation.89 | convolution fusion | flops 268435456 | bytes 13107200 | tf_op jit(solution)/shard_map/ikh,jkh->jih/dot_general | solution.py:136
  126.2 13.0 %copy.33 = bf16[128,512,64]{0,1,2:T(8,128)(2,1)} copy(bf16[128,512,64]{1,2,0:T(8,128)(2,1)} %fusion.59) | data formatting | bytes 16777216 | tf_op jit(solution)/shard_map/ikh,jkh->jih/dot_general | solution.py:136
  139.2 0.0 copy-start.15
  139.2 0.0 copy-start.17
  139.2 0.0 reduce-scatter.3.cloned.1.call-update
  139.2 0.0 copy-start.7
  139.3 0.0 copy-start.11
  139.3 0.0 copy-start.13
  139.3 0.0 all-gather.5.cloned.1.call-start
  139.3 0.5 copy-done.16
  139.9 0.1 dynamic_slice.15
  139.9 0.1 dynamic_slice.14
  140.0 0.1 compare_convert_fusion
  140.1 0.2 copy-done.4
  140.2 0.0 copy-done.12
  140.3 1.9 fusion.6
  142.1 101.5 %reduce-scatter.3.cloned.1.call-done = bf16[32,64,128]{2,0,1:T(8,128)(2,1)} async-done(((bf16[512,64,128]{2,0,1:T(8,128)(2,1)}), bf16[32,64,128]{2,0,1:T(8,128)(2,1)}) %reduce-scatter.3.cloned.1.call-update) | async-done | bytes 524304 | tf_op jit(solution)/shard_map/reduce_scatter | solution.py:135
  243.6 1.5 bitcast_reduce_fusion
  245.1 1.7 fusion.38
  246.8 2.6 fusion.58
  249.4 1.9 fusion.35
  251.4 0.0 all-gather.5.cloned.1.call-update
  251.4 0.2 reduce-scatter.5.cloned.1.call-start
  251.6 80.1 %all-gather.5.cloned.1.call-done = bf16[64,512,128]{2,1,0:T(8,128)(2,1)} async-done(((bf16[64,32,128]{2,1,0:T(8,128)(2,1)}), bf16[64,512,128]{2,1,0:T(8,128)(2,1)}) %all-gather.5.cloned.1.call-update) | async-done | bytes 8388624 | tf_op jit(solution)/shard_map/all_gather | solution.py:148
  331.8 29.2 %copy.35 = bf16[64,512,128]{0,1,2:T(8,128)(2,1)} copy(bf16[64,512,128]{2,1,0:T(8,128)(2,1)} %all-gather.5.cloned.1.call-done) | data formatting | bytes 16777216 | tf_op jit(solution)/shard_map/all_gather | solution.py:148
  360.9 10.5 %fusion.61 = bf16[128,32,512]{2,1,0:T(8,128)(2,1)} fusion(bf16[64,32,128]{0,1,2:T(8,128)(2,1)S(1)} %copy.32, bf16[64,512,128]{0,1,2:T(8,128)(2,1)} %copy.35), kind=kOutput, calls=%fused_computation.91 | convolution fusion | flops 268435456 | bytes 13107200 | tf_op jit(solution)/shard_map/ijh,ikh->jkh/dot_general | solution.py:152
  371.5 9.1 %copy.39 = bf16[128,32,512]{0,1,2:T(8,128)(2,1)} copy(bf16[128,32,512]{2,1,0:T(8,128)(2,1)} %fusion.61) | data formatting | bytes 8388608 | tf_op jit(solution)/shard_map/ijh,ikh->jkh/dot_general | solution.py:152
  380.6 0.0 reduce-scatter.5.cloned.1.call-update
  380.6 0.0 all-reduce.3.cloned.1.call-start
  380.7 1.1 copy-done.5
  381.8 1.0 fusion.7
  382.8 1.6 convolution_bitcast_fusion.2
  384.4 1.6 convolution_bitcast_fusion.1
  385.9 1.3 fusion.46
  387.2 7.4 %fusion.60 = f32[128,32,64]{2,1,0:T(8,128)S(1)} fusion(bf16[512,32,128]{0,1,2:T(8,128)(2,1)S(1)} %copy-done.1, bf16[64,512,128]{0,1,2:T(8,128)(2,1)} %copy.35), kind=kOutput, calls=%fused_computation.90 | convolution fusion | flops 268435456 | bytes 13631488 | tf_op jit(solution)/shard_map/ijh,jkh->ikh/dot_general | solution.py:149
  394.5 2.5 copy.36
  397.1 71.9 %reduce-scatter.5.cloned.1.call-done = bf16[64,32,128]{2,1,0:T(8,128)(2,1)} async-done(((bf16[512,32,128]{2,1,0:T(8,128)(2,1)}), bf16[64,32,128]{2,1,0:T(8,128)(2,1)}) %reduce-scatter.5.cloned.1.call-update) | async-done | bytes 524304 | tf_op jit(solution)/shard_map/reduce_scatter | solution.py:151
  469.0 3.2 multiply_convert_fusion.3
  472.2 0.0 copy-start.9
  472.2 0.8 copy-done.10
  473.0 1.8 convolution_bitcast_fusion
  474.8 2.5 fusion.57
  477.3 0.0 all-reduce.3.cloned.1.call-update
  477.4 1.9 fusion.18
  479.3 144.0 %all-reduce.3.cloned.1.call-done = (f32[128,512]{1,0:T(8,128)}, f32[128,128]{1,0:T(8,128)}, f32[128,128]{1,0:T(8,128)}) async-done(((f32[128,512]{1,0:T(8,128)}, f32[128,128]{1,0:T(8,128)}, f32[128,128]{1,0:T(8,128)}), (f32[128,512]{1,0:T(8,128)}, f32[128,128]{1,0:T(8,128)}, f32[128,128]{1,0:T(8,128)})) %all-reduce.3.cloned.1.call-update) | async-done | bytes 393232 | tf_op jit(solution)/shard_map/psum | solution.py:172
  623.3 1.7 broadcast_multiply_fusion
  625.0 1.5 broadcast_multiply_fusion.2
  626.5 1.5 broadcast_multiply_fusion.1
  (32 shorter events, 0.1 us)
Async XLA Ops:
  7.2 4.1 copy-start
  7.2 102.6 %all-gather.3.cloned.1.call-start = ((), (), s32[]{:S(2)}) async-start(), calls=%async_computation.2 | async-start | bytes 4718592 | tf_op jit(solution)/shard_map/all_gather | solution.py:132
  13.3 2.0 copy-start.2
  16.6 227.0 %reduce-scatter.3.cloned.1.call-start = ((), (), s32[]{:S(2)}) async-start(), calls=%async_computation.3 | async-start | bytes 8912896 | tf_op jit(solution)/shard_map/reduce_scatter | solution.py:135
  139.2 0.7 copy-start.16
  139.2 1.1 copy-start.4
  139.2 1.1 copy-start.12
  139.2 1.1 copy-start.14
  139.2 1.1 copy-start.15
  139.2 1.0 copy-start.17
  139.2 107.5 %copy-start.7 = (bf16[64,32,128]{2,1,0:T(8,128)(2,1)S(1)}, bf16[64,32,128]{2,1,0:T(8,128)(2,1)}, u32[]{:S(2)}) copy-start(bf16[64,32,128]{2,1,0:T(8,128)(2,1)} %param.13) | copy-start | bytes 1572868
  139.3 107.5 %copy-start.11 = (bf16[128,128]{1,0:T(8,128)(2,1)S(1)}, bf16[128,128]{1,0:T(8,128)(2,1)}, u32[]{:S(2)}) copy-start(bf16[128,128]{1,0:T(8,128)(2,1)} %param.23) | copy-start | bytes 98308
  139.3 107.5 %copy-start.13 = (f32[128]{0:T(128)S(1)}, f32[128]{0:T(128)}, u32[]{:S(2)}) copy-start(f32[128]{0:T(128)} %param.21) | copy-start | bytes 1540
  139.3 192.5 %all-gather.5.cloned.1.call-start = ((), (), s32[]{:S(2)}) async-start(), calls=%async_computation.4 | async-start | bytes 8912896 | tf_op jit(solution)/shard_map/all_gather | solution.py:148
  243.6 5.8 copy-start.3
  251.4 217.6 %reduce-scatter.5.cloned.1.call-start = ((), (), s32[]{:S(2)}) async-start(), calls=%async_computation.5 | async-start | bytes 4718592 | tf_op jit(solution)/shard_map/reduce_scatter | solution.py:151
  380.6 1.2 copy-start.5
  380.6 1.2 copy-start.18
  380.6 242.7 %all-reduce.3.cloned.1.call-start = ((), (), s32[]{:S(2)}) async-start(), calls=%async_computation.6 | async-start | bytes 786432 | tf_op jit(solution)/shard_map/psum | solution.py:172
  382.8 4.4 copy-start.1
  472.2 0.8 copy-start.10
  472.2 2.6 copy-start.8
  472.2 2.6 copy-start.9
  473.0 1.8 copy-start.6
Sparse Core Ops, SparseCore 0:
  16.7 92.9 all-gather.2
  139.4 104.1 reduce-scatter.2
  251.5 80.1 all-gather.4
  380.7 88.1 reduce-scatter.4
  477.5 145.7 all-reduce.2
where the time goes:
time: 636 us; the launch traced here: 634 us
  waiting for transfers between devices  489 us (77%)
  local copies, waits for them, and re-layouts  69.1 us (11%)
  matrix products  41.8 us (7%)
  other arithmetic  20.2 us (3%)
  between operations  14.1 us (2%)
    psum x1, waiting for transfers between devices, body(): sums = lax.psum((term_proj, term_gate, term_out), ('row', 'col'))  144 us
    reduce_scatter x1, waiting for transfers between devices, body(): lax.psum_scatter(jnp.einsum('ikh,jkh->jih', act_a, piece, preferred_eleme...  101 us
    all_gather x1, waiting for transfers between devices, body(): b_cols = lax.all_gather(act_b, 'row', axis=0, tiled=True)  91.4 us
    all_gather x1, waiting for transfers between devices, body(): dx_rows = lax.all_gather(grad_mixed, 'col', axis=1, tiled=True)  80.1 us
    reduce_scatter x1, waiting for transfers between devices, body(): lax.psum_scatter(jnp.einsum('ijh,ikh->jkh', piece, act_a, preferred_eleme...  71.9 us
    all_gather x1, local copies, waits for them, and re-layouts, body(): dx_rows = lax.all_gather(grad_mixed, 'col', axis=1, tiled=True)  29.2 us
    dot_general x1, local copies, waits for them, and re-layouts, body(): jnp.einsum('ikh,jkh->jih', act_a, piece, preferred_element_type=jnp.float32)  13 us
  transfers between devices with their start and end apart: 5, of which 5 were waited for; matrix products, arithmetic and copies ran while one was open for 3% of the time, Pallas kernels for 0%

commit v1 on v0

--- a/solution.py
+++ b/solution.py
@@ -129,7 +129,9 @@
     same = (chain_rows[:, None] == chain_cols[None, :]).astype(jnp.float32)[:, :, None]
     normed_b, normed, inverse, proj = project(pair, ln_in_gain, ln_in_bias, w_proj)
     act_a, act_b = activations(proj, pair_mask)
-    b_cols = lax.all_gather(act_b, "row", axis=0, tiled=True)
+    b_cols = jnp.concatenate(
+        lax.all_to_all(jnp.stack([act_b] * lax.axis_size("row")), "row", 0, 0), axis=0
+    )
     piece = b_cols
     mixed = jnp.transpose(
         lax.psum_scatter(

time: 636 us -> 609 us (0.958)
  waiting for transfers between devices: 489 us -> 454 us
    all_gather x1 -> x0, waiting for transfers between devices: 91.4 us -> none  [body(): b_cols = lax.all_gather(act_b, 'row', axis=0, tiled=True)]
    all_to_all x0 -> x1, waiting for transfers between devices: none -> 57.2 us  [body(): lax.all_to_all(jnp.stack([act_b] * lax.axis_size('row')), 'row', 0, 0)]
    reshape x0 -> x1, local copies, waits for them, and re-layouts: none -> 8.59 us  [body(): jnp.concatenate(lax.all_to_all(jnp.stack([act_b] * lax.axis_size('row')),...]
    all_gather x1 -> x0, local copies, waits for them, and re-layouts: 8.59 us -> none  [body(): b_cols = lax.all_gather(act_b, 'row', axis=0, tiled=True)]
where the time goes in v1:
time: 609 us; the launch traced here: 607 us
  waiting for transfers between devices  454 us (75%)
  local copies, waits for them, and re-layouts  71.7 us (12%)
  matrix products  41.8 us (7%)
  other arithmetic  19.4 us (3%)
  between operations  14.1 us (2%)
  starting transfers between devices  6.54 us (1%)
    psum x1, waiting for transfers between devices, body(): sums = lax.psum((term_proj, term_gate, term_out), ('row', 'col'))  144 us
    reduce_scatter x1, waiting for transfers between devices, body(): lax.psum_scatter(jnp.einsum('ikh,jkh->jih', act_a, piece, preferred_eleme...  100 us
    all_gather x1, waiting for transfers between devices, body(): dx_rows = lax.all_gather(grad_mixed, 'col', axis=1, tiled=True)  80.3 us
    reduce_scatter x1, waiting for transfers between devices, body(): lax.psum_scatter(jnp.einsum('ijh,ikh->jkh', piece, act_a, preferred_eleme...  71.9 us
    all_to_all x1, waiting for transfers between devices, body(): lax.all_to_all(jnp.stack([act_b] * lax.axis_size('row')), 'row', 0, 0)  57.2 us
    all_gather x1, local copies, waits for them, and re-layouts, body(): dx_rows = lax.all_gather(grad_mixed, 'col', axis=1, tiled=True)  29.1 us
    dot_general x1, local copies, waits for them, and re-layouts, body(): jnp.einsum('ikh,jkh->jih', act_a, piece, preferred_element_type=jnp.float32)  13 us
  transfers between devices with their start and end apart: 5, of which 5 were waited for; matrix products, arithmetic and copies ran while one was open for 3% of the time, Pallas kernels for 0%

profile of v1, /device:TPU:1, one launch (start us, length us, event | category | flops | bytes accessed | tf_op | source)
XLA Modules:
  0.0 607.3 jit_solution(6065019327762495673)
XLA Ops:
  7.2 0.0 copy-start
  7.2 0.7 convert_element_type.61
  7.9 0.1 dynamic_slice.13
  8.0 0.1 dynamic_slice.12
  8.1 1.4 convert_reduce_fusion
  9.5 1.7 fusion.19
  11.2 0.1 broadcast_multiply_fusion.3
  11.2 2.0 fusion.42
  13.2 2.0 copy-done.2
  15.2 0.6 multiply_convert_fusion.4
  15.8 2.7 stack.2
  18.5 6.2 %all-to-all-start = ((bf16[8,64,32,128]{3,2,1,0:T(8,128)(2,1)}), bf16[8,64,32,128]{3,2,1,0:T(8,128)(2,1)}, u32[]{:S(2)}, u32[]{:S(2)}) async-start(bf16[8,64,32,128]{3,2,1,0:T(8,128)(2,1)} %stack.2), calls=%async_computation | async-start | bytes 8388608 | tf_op jit(solution)/shard_map/all_to_all | solution.py:133
  24.7 0.0 reduce-scatter.3.cloned.1.call-start
  24.8 1.7 copy.31
  26.5 57.2 %all-to-all-done = bf16[8,64,32,128]{3,2,1,0:T(8,128)(2,1)} async-done(((bf16[8,64,32,128]{3,2,1,0:T(8,128)(2,1)}), bf16[8,64,32,128]{3,2,1,0:T(8,128)(2,1)}, u32[]{:S(2)}, u32[]{:S(2)}) %all-to-all-start) | async-done | bytes 4194336 | tf_op jit(solution)/shard_map/all_to_all | solution.py:133
  83.6 8.6 %copy.33 = bf16[512,32,128]{0,1,2:T(8,128)(2,1)} copy(bf16[512,32,128]{2,1,0:T(8,128)(2,1)} %bitcast.1) | data formatting | bytes 8388608 | tf_op jit(solution)/shard_map/reshape | solution.py:132
  92.2 7.8 %fusion.59 = bf16[128,512,64]{1,2,0:T(8,128)(2,1)} fusion(bf16[512,32,128]{0,1,2:T(8,128)(2,1)} %copy.33, bf16[64,32,128]{0,1,2:T(8,128)(2,1)S(1)} %copy.31), kind=kOutput, calls=%fused_computation.89 | convolution fusion | flops 268435456 | bytes 13107200 | tf_op jit(solution)/shard_map/ikh,jkh->jih/dot_general | solution.py:138
  100.0 13.0 %copy.32 = bf16[128,512,64]{0,1,2:T(8,128)(2,1)} copy(bf16[128,512,64]{1,2,0:T(8,128)(2,1)} %fusion.59) | data formatting | bytes 16777216 | tf_op jit(solution)/shard_map/ikh,jkh->jih/dot_general | solution.py:138
  113.0 0.0 copy-start.15
  113.0 0.0 copy-start.17
  113.0 0.0 reduce-scatter.3.cloned.1.call-update
  113.1 0.0 copy-start.7
  113.1 0.0 copy-start.11
  113.1 0.0 copy-start.13
  113.1 0.0 all-gather.2.cloned.1.call-start
  113.2 0.5 copy-done.16
  113.7 0.1 dynamic_slice.15
  113.8 0.1 dynamic_slice.14
  113.8 0.1 compare_convert_fusion
  113.9 0.2 copy-done.4
  114.1 0.0 copy-done.12
  114.1 1.9 fusion.6
  115.9 100.3 %reduce-scatter.3.cloned.1.call-done = bf16[32,64,128]{2,0,1:T(8,128)(2,1)} async-done(((bf16[512,64,128]{2,0,1:T(8,128)(2,1)}), bf16[32,64,128]{2,0,1:T(8,128)(2,1)}) %reduce-scatter.3.cloned.1.call-update) | async-done | bytes 524304 | tf_op jit(solution)/shard_map/reduce_scatter | solution.py:137
  216.3 1.5 bitcast_reduce_fusion
  217.7 1.7 fusion.38
  219.5 2.6 fusion.58
  222.1 1.9 fusion.35
  224.0 0.0 all-gather.2.cloned.1.call-update
  224.0 0.2 reduce-scatter.5.cloned.1.call-start
  224.3 80.3 %all-gather.2.cloned.1.call-done = bf16[64,512,128]{2,1,0:T(8,128)(2,1)} async-done(((bf16[64,32,128]{2,1,0:T(8,128)(2,1)}), bf16[64,512,128]{2,1,0:T(8,128)(2,1)}) %all-gather.2.cloned.1.call-update) | async-done | bytes 8388624 | tf_op jit(solution)/shard_map/all_gather | solution.py:150
  304.5 29.1 %copy.34 = bf16[64,512,128]{0,1,2:T(8,128)(2,1)} copy(bf16[64,512,128]{2,1,0:T(8,128)(2,1)} %all-gather.2.cloned.1.call-done) | data formatting | bytes 16777216 | tf_op jit(solution)/shard_map/all_gather | solution.py:150
  333.7 10.5 %fusion.61 = bf16[128,32,512]{2,1,0:T(8,128)(2,1)} fusion(bf16[64,32,128]{0,1,2:T(8,128)(2,1)S(1)} %copy.31, bf16[64,512,128]{0,1,2:T(8,128)(2,1)} %copy.34), kind=kOutput, calls=%fused_computation.91 | convolution fusion | flops 268435456 | bytes 13107200 | tf_op jit(solution)/shard_map/ijh,ikh->jkh/dot_general | solution.py:154
  344.2 9.1 %copy.38 = bf16[128,32,512]{0,1,2:T(8,128)(2,1)} copy(bf16[128,32,512]{2,1,0:T(8,128)(2,1)} %fusion.61) | data formatting | bytes 8388608 | tf_op jit(solution)/shard_map/ijh,ikh->jkh/dot_general | solution.py:154
  353.3 0.0 reduce-scatter.5.cloned.1.call-update
  353.4 0.0 all-reduce.3.cloned.1.call-start
  353.4 1.1 copy-done.5
  354.6 1.0 fusion.7
  355.5 1.6 convolution_bitcast_fusion.2
  357.1 1.6 convolution_bitcast_fusion.1
  358.7 1.3 fusion.46
  359.9 7.4 %fusion.60 = f32[128,32,64]{2,1,0:T(8,128)S(1)} fusion(bf16[512,32,128]{0,1,2:T(8,128)(2,1)S(1)} %copy-done.1, bf16[64,512,128]{0,1,2:T(8,128)(2,1)} %copy.34), kind=kOutput, calls=%fused_computation.90 | convolution fusion | flops 268435456 | bytes 13631488 | tf_op jit(solution)/shard_map/ijh,jkh->ikh/dot_general | solution.py:151
  367.3 2.5 copy.35
  369.8 71.9 %reduce-scatter.5.cloned.1.call-done = bf16[64,32,128]{2,1,0:T(8,128)(2,1)} async-done(((bf16[512,32,128]{2,1,0:T(8,128)(2,1)}), bf16[64,32,128]{2,1,0:T(8,128)(2,1)}) %reduce-scatter.5.cloned.1.call-update) | async-done | bytes 524304 | tf_op jit(solution)/shard_map/reduce_scatter | solution.py:153
  441.7 3.2 multiply_convert_fusion.3
  444.9 0.0 copy-start.9
  444.9 0.8 copy-done.10
  445.7 1.8 convolution_bitcast_fusion
  447.5 2.5 fusion.57
  450.1 0.0 all-reduce.3.cloned.1.call-update
  450.1 1.9 fusion.18
  452.0 144.1 %all-reduce.3.cloned.1.call-done = (f32[128,512]{1,0:T(8,128)}, f32[128,128]{1,0:T(8,128)}, f32[128,128]{1,0:T(8,128)}) async-done(((f32[128,512]{1,0:T(8,128)}, f32[128,128]{1,0:T(8,128)}, f32[128,128]{1,0:T(8,128)}), (f32[128,512]{1,0:T(8,128)}, f32[128,128]{1,0:T(8,128)}, f32[128,128]{1,0:T(8,128)})) %all-reduce.3.cloned.1.call-update) | async-done | bytes 393232 | tf_op jit(solution)/shard_map/psum | solution.py:174
  596.1 1.7 broadcast_multiply_fusion
  597.8 1.5 broadcast_multiply_fusion.2
  599.3 1.5 broadcast_multiply_fusion.1
  (32 shorter events, 0.1 us)
Async XLA Ops:
  7.2 4.1 copy-start
  13.2 2.0 copy-start.2
  18.5 65.1 %all-to-all-start = ((bf16[8,64,32,128]{3,2,1,0:T(8,128)(2,1)}), bf16[8,64,32,128]{3,2,1,0:T(8,128)(2,1)}, u32[]{:S(2)}, u32[]{:S(2)}) async-start(bf16[8,64,32,128]{3,2,1,0:T(8,128)(2,1)} %stack.2), calls=%async_computation | async-start | bytes 8388608 | tf_op jit(solution)/shard_map/all_to_all | solution.py:133
  24.7 191.6 %reduce-scatter.3.cloned.1.call-start = ((), (), s32[]{:S(2)}) async-start(), calls=%async_computation.3 | async-start | bytes 8912896 | tf_op jit(solution)/shard_map/reduce_scatter | solution.py:137
  113.0 0.7 copy-start.16
  113.0 1.1 copy-start.4
  113.0 1.1 copy-start.12
  113.0 1.1 copy-start.14
  113.0 1.1 copy-start.15
  113.0 1.0 copy-start.17
  113.1 106.4 %copy-start.7 = (bf16[64,32,128]{2,1,0:T(8,128)(2,1)S(1)}, bf16[64,32,128]{2,1,0:T(8,128)(2,1)}, u32[]{:S(2)}) copy-start(bf16[64,32,128]{2,1,0:T(8,128)(2,1)} %param.13) | copy-start | bytes 1572868
  113.1 106.4 %copy-start.11 = (bf16[128,128]{1,0:T(8,128)(2,1)S(1)}, bf16[128,128]{1,0:T(8,128)(2,1)}, u32[]{:S(2)}) copy-start(bf16[128,128]{1,0:T(8,128)(2,1)} %param.23) | copy-start | bytes 98308
  113.1 106.4 %copy-start.13 = (f32[128]{0:T(128)S(1)}, f32[128]{0:T(128)}, u32[]{:S(2)}) copy-start(f32[128]{0:T(128)} %param.21) | copy-start | bytes 1540
  113.1 191.4 %all-gather.2.cloned.1.call-start = ((), (), s32[]{:S(2)}) async-start(), calls=%async_computation.4 | async-start | bytes 8912896 | tf_op jit(solution)/shard_map/all_gather | solution.py:150
  216.3 5.8 copy-start.3
  224.0 217.7 %reduce-scatter.5.cloned.1.call-start = ((), (), s32[]{:S(2)}) async-start(), calls=%async_computation.5 | async-start | bytes 4718592 | tf_op jit(solution)/shard_map/reduce_scatter | solution.py:153
  353.3 1.2 copy-start.5
  353.3 1.2 copy-start.18
  353.4 242.8 %all-reduce.3.cloned.1.call-start = ((), (), s32[]{:S(2)}) async-start(), calls=%async_computation.6 | async-start | bytes 786432 | tf_op jit(solution)/shard_map/psum | solution.py:174
  355.5 4.4 copy-start.1
  444.9 0.8 copy-start.10
  444.9 2.6 copy-start.8
  444.9 2.6 copy-start.9
  445.7 1.8 copy-start.6
Sparse Core Ops, SparseCore 0:
  113.2 103.0 reduce-scatter.2
  224.2 80.3 all-gather.1
  353.5 88.1 reduce-scatter.4
  450.2 145.8 all-reduce.2
